TPU v7x, 128 devices: a whole 4x4x4 slice. The times are simulated.
128 devices in a mesh: dp: 16 (over x, y), mp: 8 (over z, core).
Axes of the slice: x: 4, y: 4, z: 4, core: 2. Of those that a mesh axis runs over, the one named last changes fastest.
Arguments:
- patches: bfloat16 [4096, 6144], P('dp', 'mp'), may hold values from -6 to 6
- dest_group: int32 [4096], P('dp'), may hold values from 0 to 15, as said below
- dest_row: int32 [4096], P('dp'), may hold values from 0 to 255, as said below
- segment: int32 [4096], P('dp'), may hold values from 0 to 31, as said below
- ln_gain: float32 [6144], replicated, may hold values from 0.1 to 1.9
- w_qkv: bfloat16 [6144, 3, 3072], P(None, None, 'mp'), may hold values from -0.078125 to 0.078125
- qk_gain: float32 [2, 128], replicated, may hold values from 0.1 to 1.9
- w_out: bfloat16 [6144, 3072], P(None, 'mp'), may hold values from -0.4375 to 0.4375
- cotangent: bfloat16 [4096, 6144], P('dp', 'mp'), may hold values from -6 to 6
Outputs:
- output: bfloat16 [4096, 6144], P('dp', 'mp')
- input_grad: bfloat16 [4096, 6144], P('dp', 'mp')
- qkv_grad: bfloat16 [6144, 3, 3072], P('dp', None, 'mp')
- out_grad: bfloat16 [6144, 3072], P('dp', 'mp')
Inputs may be any that keep to these rules, and one draw needn't show every extreme that they name: The pairs (dest_group, dest_row) of all rows name every row of every group exactly once. The rows of one group send at most 32 rows to any one group, and in every draw some group sends exactly 32 rows to some group. `dest_row`: see dest_group. `segment`: rows of one group with equal numbers are one image and stand in consecutive rows; numbers lie between 0 and 31.
All inputs are finite; a program needn't handle non-finite values.
Results may differ from a plain program's by a relative error of at most 0.024.
Values may be sent and summed in bfloat16 or wider, within the bound.
A program may use at most 192 MiB of HBM per device.

v0:
```python
import math
import jax
import jax.numpy as jnp
from jax import lax
from jax.sharding import PartitionSpec as P

DH = 128


def norm_heads(values, gain):
    center = values - jnp.mean(values, -1, keepdims=True)
    variance = jnp.mean(center * center, -1, keepdims=True)
    return center * lax.rsqrt(variance + 1e-06) * gain


def attend(projected, image_ids, qk_gain):
    row_count = projected.shape[0]
    head_count = projected.shape[2] // DH
    split_heads = projected.reshape(row_count, 3, head_count, DH)
    queries = norm_heads(split_heads[:, 0], qk_gain[0]).astype(jnp.bfloat16)
    keys_normed = norm_heads(split_heads[:, 1], qk_gain[1]).astype(jnp.bfloat16)
    values_bf = split_heads[:, 2].astype(jnp.bfloat16)
    scores = jnp.einsum(
        "qhd,khd->hqk", queries, keys_normed, preferred_element_type=jnp.float32
    ) * DH ** (-0.5)
    same_image = image_ids[:, None] == image_ids[None, :]
    raised = jnp.where(same_image[None], jnp.exp(scores), 0.0)
    weights = (raised / jnp.sum(raised, -1, keepdims=True)).astype(jnp.bfloat16)
    mixed = jnp.einsum("hqk,khd->qhd", weights, values_bf, preferred_element_type=jnp.float32)
    return mixed.reshape(row_count, head_count * DH).astype(jnp.bfloat16)


def contract_rows(left, right):
    return lax.dot_general(
        left, right, (((0,), (0,)), ((), ())), preferred_element_type=jnp.float32
    )


def contract_cols(left, right):
    return lax.dot_general(
        left, right, (((1,), (1,)), ((), ())), preferred_element_type=jnp.float32
    )


def shards(patches, dest_group, dest_row, segment, ln_gain, w_qkv, qk_gain, w_out, cotangent):
    group_rows, part_width = patches.shape
    groups = lax.axis_size("dp")
    slot_size = 2 * group_rows // groups
    full_width, local_width = w_out.shape
    member = (dest_group[:, None] == jnp.arange(groups, dtype=jnp.int32)[None, :]).astype(jnp.int32)
    rank_within = jnp.sum((jnp.cumsum(member, 0) - 1) * member, 1)
    place = dest_group * slot_size + rank_within
    outbox = jnp.zeros((groups * slot_size, part_width), patches.dtype).at[place].set(patches)
    address = jnp.full((groups * slot_size,), group_rows, jnp.int32).at[place].set(dest_row)
    inbox, arrived_at = (
        lax.all_to_all(
            outbox.reshape(groups, slot_size, part_width),
            "dp",
            split_axis=0,
            concat_axis=0,
            tiled=True,
        ),
        lax.all_to_all(
            address.reshape(groups, slot_size), "dp", split_axis=0, concat_axis=0, tiled=True
        ),
    )
    packed = (
        jnp.zeros((group_rows, part_width), patches.dtype)
        .at[arrived_at.reshape(-1)]
        .set(inbox.reshape(-1, part_width), mode="drop")
    )
    whole_rows, whole_cot = (
        lax.all_gather(packed, "mp", axis=1, tiled=True),
        lax.all_gather(cotangent, "mp", axis=1, tiled=True),
    )
    wide = whole_rows.astype(jnp.float32)
    center = wide - jnp.mean(wide, -1, keepdims=True)
    rstd = lax.rsqrt(jnp.mean(center * center, -1, keepdims=True) + 1e-06)
    unit_rows = center * rstd
    normed = (unit_rows * ln_gain).astype(jnp.bfloat16)
    w_flat = w_qkv.reshape(full_width, 3 * local_width)
    projected = jnp.dot(normed, w_flat, preferred_element_type=jnp.float32).reshape(
        group_rows, 3, local_width
    )
    heads_out, backward = jax.vjp(lambda values: attend(values, segment, qk_gain), projected)
    attn = lax.psum_scatter(
        contract_cols(heads_out, w_out).astype(jnp.bfloat16), "mp", scatter_dimension=1, tiled=True
    ).astype(jnp.float32)
    output = (packed.astype(jnp.float32) + attn).astype(jnp.bfloat16)
    d_heads = jnp.dot(whole_cot, w_out, preferred_element_type=jnp.float32).astype(jnp.bfloat16)
    (d_projected,) = backward(d_heads)
    d_proj_bf = d_projected.astype(jnp.bfloat16).reshape(group_rows, 3 * local_width)
    d_part = contract_cols(d_proj_bf, w_flat)
    my_index = lax.axis_index("mp")
    d_normed = lax.psum(d_part.astype(jnp.bfloat16), "mp").astype(jnp.float32)
    d_unit = d_normed * ln_gain
    d_full = rstd * (
        d_unit
        - jnp.mean(d_unit, -1, keepdims=True)
        - unit_rows * jnp.mean(d_unit * unit_rows, -1, keepdims=True)
    )
    d_input = lax.dynamic_slice_in_dim(d_full, my_index * part_width, part_width, 1)
    input_grad = (cotangent.astype(jnp.float32) + d_input).astype(jnp.bfloat16)
    sum_qkv, sum_out = (
        lax.psum_scatter(
            contract_rows(normed, d_proj_bf).astype(jnp.bfloat16),
            "dp",
            scatter_dimension=0,
            tiled=True,
        ).astype(jnp.float32),
        lax.psum_scatter(
            contract_rows(whole_cot, heads_out).astype(jnp.bfloat16),
            "dp",
            scatter_dimension=0,
            tiled=True,
        ).astype(jnp.float32),
    )
    scale_grad = 1.0 / math.sqrt(group_rows * groups)
    qkv_grad = (sum_qkv * scale_grad).reshape(-1, 3, local_width).astype(jnp.bfloat16)
    out_grad = (sum_out * scale_grad).astype(jnp.bfloat16)
    return (output, input_grad, qkv_grad, out_grad)


def solution(mesh):
    placed = (
        P("dp", "mp"),
        P("dp"),
        P("dp"),
        P("dp"),
        P(),
        P(None, None, "mp"),
        P(),
        P(None, "mp"),
        P("dp", "mp"),
    )
    return jax.shard_map(
        shards,
        mesh=mesh,
        in_specs=placed,
        out_specs=(P("dp", "mp"), P("dp", "mp"), P("dp", None, "mp"), P("dp", "mp")),
        check_vma=False,
    )
```

profile of v0, /device:TPU:1, one launch (start us, length us, event | category | flops | bytes accessed | tf_op | source)
XLA Modules:
  0.0 402.0 jit_solution(2269803845035048360)
XLA Ops:
  7.2 0.0 all-gather.5.cloned.1.call-start
  7.2 0.7 all-gather.5.cloned.1.call-update
  7.9 0.7 fusion.32
  8.6 0.6 reduce-window.6
  9.2 0.2 slice_reduce_fusion.2
  9.4 0.8 fusion.31
  10.2 0.7 compare_select_fusion.1
  10.8 1.6 scatter_custom_fusion
  12.4 0.7 all_to_all.9
  13.1 7.6 %all-to-all-start = ((s32[16,1,32]{2,1,0:T(1,128)}), s32[16,1,32]{2,1,0:T(1,128)S(1)}, u32[]{:S(2)}, u32[]{:S(2)}) async-start(s32[16,1,32]{2,1,0:T(1,128)} %all_to_all.9), calls=%async_computation | async-start | bytes 16384 | tf_op jit(solution)/shard_map/all_to_all | solution.py:63
  20.7 3.1 scatter_custom_fusion.1
  23.7 3.3 all-to-all-done
  27.0 3.6 all-to-all-start.1
  30.6 0.0 all-gather.3.cloned.1.call-start
  30.7 0.5 broadcast.243
  31.2 0.7 reduce.7
  31.9 0.1 reshape.195
  32.0 10.6 %all-to-all-done.1 = bf16[16,32,768]{2,1,0:T(8,128)(2,1)S(1)} async-done(((bf16[16,32,768]{2,1,0:T(8,128)(2,1)}), bf16[16,32,768]{2,1,0:T(8,128)(2,1)S(1)}, u32[]{:S(2)}, u32[]{:S(2)}) %all-to-all-start.1) | async-done | bytes 786464 | tf_op jit(solution)/shard_map/all_to_all | solution.py:56
  42.6 3.3 scatter_custom_fusion.2
  45.9 0.2 all-reduce.5.cloned.1.call-start
  46.2 18.8 %copy.39 = bf16[6144,3,384]{0,2,1:T(8,128)(2,1)} copy(bf16[6144,3,384]{2,0,1:T(8,128)(2,1)} %param.14) | data formatting | bytes 28311552 | tf_op args[5]
  64.9 0.1 broadcast_compare_fusion
  65.1 0.0 all-gather.5.cloned.1.call-done
  65.1 5.2 %convolution_convert_fusion.5 = bf16[256,384]{1,0:T(8,128)(2,1)S(1)} fusion(bf16[256,6144]{1,0:T(8,128)(2,1)} %all-gather.5.cloned.1.call-done, bf16[6144,384]{1,0:T(8,128)(2,1)} %param.16), kind=kOutput, calls=%fused_computation.27 | convolution fusion | flops 1208057856 | bytes 8060928 | tf_op jit(solution)/shard_map/dot_general | solution.py:90
  70.3 0.1 copy.43
  70.5 5.5 %all-gather.3.cloned.1.call-done = bf16[256,6144]{1,0:T(8,128)(2,1)} async-done(((bf16[256,768]{1,0:T(8,128)(2,1)}), bf16[256,6144]{1,0:T(8,128)(2,1)}) %all-gather.3.cloned.1.call-update) | async-done | bytes 3145744 | tf_op jit(solution)/shard_map/all_gather | solution.py:73
  76.0 2.5 convert_reduce_fusion
  78.6 0.3 copy-done
  78.9 1.0 fusion.4
  79.8 7.3 %fusion.5 = f32[256,3,3,128]{0,3,2,1:T(8,128)S(1)} fusion(bf16[3,3,128,6144]{3,2,1,0:T(8,128)(2,1)} %bitcast.122, f32[6144]{0:T(1024)S(1)} %copy-done.5, bf16[256,6144]{1,0:T(8,128)(2,1)S(1)} %copy-done, f32[256]{0:T(256)S(1)} %add_rsqrt_fusion, f32[256]{0:T(256)S(1)} %broadcast_multiply_fusion.4), kind=kOutput, calls=%fused_computation.17 | convolution fusion | flops 3631742976 | bytes 18507776 | tf_op jit(solution)/shard_map/dot_general | solution.py:82
  87.2 0.1 slice_reduce_fusion
  87.3 0.1 multiply_reduce_fusion.4
  87.4 0.5 select_reduce_fusion
  87.9 0.3 fusion.16
  88.2 0.4 multiply_reduce_fusion.1
  88.6 0.4 multiply_reduce_fusion.3
  89.0 0.4 fusion.28
  89.5 0.2 add_bitcast_fusion.1
  89.7 0.1 add_bitcast_fusion
  89.8 0.9 add_convert_fusion
  90.6 11.2 %fusion = bf16[256,6144]{1,0:T(8,128)(2,1)} fusion(bf16[256,3,384]{0,2,1:T(8,128)(2,1)} %bitcast.124, bf16[6144,3,384]{2,0,1:T(8,128)(2,1)} %param.14), kind=kOutput, calls=%fused_computation.8 | convolution fusion | flops 3625451520 | bytes 17891328 | tf_op jit(solution)/shard_map/dot_general | solution.py:40
  101.8 0.0 all-reduce.5.cloned.1.call-update
  101.8 0.3 reduce-scatter.6.cloned.1.call-start
  102.1 1.5 convolution_convert_fusion.6
  103.6 5.9 %convolution_convert_fusion.2 = bf16[256,6144]{1,0:T(8,128)(2,1)} fusion(bf16[256,384]{0,1:T(8,128)(2,1)S(1)} %bitcast.129, bf16[6144,384]{1,0:T(8,128)(2,1)} %param.16), kind=kOutput, calls=%fused_computation.10 | convolution fusion | flops 1209532416 | bytes 8060928 | tf_op jit(solution)/shard_map/dot_general | solution.py:40
  109.6 0.0 reduce-scatter.6.cloned.1.call-update
  109.6 0.0 reduce-scatter.10.cloned.1.call-start
  109.6 5.5 %fusion.1 = bf16[6144,384]{0,1:T(8,128)(2,1)} fusion(bf16[256,384]{0,1:T(8,128)(2,1)S(1)} %bitcast.130, bf16[256,6144]{1,0:T(8,128)(2,1)} %all-gather.5.cloned.1.call-done), kind=kOutput, calls=%fused_computation.9 | convolution fusion | flops 1210318848 | bytes 8060928 | tf_op jit(solution)/shard_map/dot_general | solution.py:34
  115.1 6.7 %copy.61 = bf16[6144,384]{1,0:T(8,128)(2,1)} copy(bf16[6144,384]{0,1:T(8,128)(2,1)} %fusion.1) | data formatting | bytes 9437184
  121.9 0.0 reduce-scatter.8.cloned.1.call-start
  121.9 8.9 %convolution_convert_fusion = bf16[6144,1152]{1,0:T(8,128)(2,1)} fusion(bf16[256,1152]{0,1:T(8,128)(2,1)} %bitcast.125, f32[6144]{0:T(1024)S(1)} %copy-done.5, bf16[256,6144]{1,0:T(8,128)(2,1)S(1)} %copy-done, f32[256]{0:T(256)S(1)} %add_rsqrt_fusion, f32[256]{0:T(256)S(1)} %broadcast_multiply_fusion.4), kind=kOutput, calls=%fused_computation.3 | convolution fusion | flops 3638820864 | bytes 17917952 | tf_op jit(solution)/shard_map/dot_general | solution.py:34
  130.9 38.0 %all-reduce.5.cloned.1.call-done = bf16[256,6144]{1,0:T(8,128)(2,1)} async-done(((bf16[256,6144]{1,0:T(8,128)(2,1)}), bf16[256,6144]{1,0:T(8,128)(2,1)}) %all-reduce.5.cloned.1.call-update) | async-done | bytes 3145744 | tf_op jit(solution)/shard_map/psum | solution.py:95
  168.9 4.1 %fusion.7 = (f32[256]{0:T(256)S(1)}, f32[256]{0:T(256)S(1)}, f32[256,6144]{1,0:T(8,128)S(1)}, f32[256,6144]{1,0:T(8,128)S(1)}) fusion(f32[6144]{0:T(1024)} %param.13, bf16[256,6144]{1,0:T(8,128)(2,1)} %all-reduce.5.cloned.1.call-done, f32[256]{0:T(256)S(1)} %add_rsqrt_fusion, f32[256]{0:T(256)S(1)} %broadcast_multiply_fusion.4, bf16[256,6144]{1,0:T(8,128)(2,1)S(1)} %copy-done), kind=kLoop, calls=%fused_computation.19 | loop fusion | flops 12582400 | bytes 18903040 | tf_op jit(solution)/shard_map/reduce_sum | solution.py:99
  173.1 1.0 fusion.20
  174.1 31.3 %reduce-scatter.6.cloned.1.call-done = bf16[256,768]{1,0:T(8,128)(2,1)} async-done(((bf16[256,6144]{1,0:T(8,128)(2,1)}), bf16[256,768]{1,0:T(8,128)(2,1)}) %reduce-scatter.6.cloned.1.call-update) | async-done | bytes 393232 | tf_op jit(solution)/shard_map/reduce_scatter | solution.py:86
  205.4 1.8 add_convert_fusion.1
  207.2 79.7 %reduce-scatter.10.cloned.1.call-done = bf16[384,384]{1,0:T(8,128)(2,1)} async-done(((bf16[6144,384]{1,0:T(8,128)(2,1)}), bf16[384,384]{1,0:T(8,128)(2,1)}) %reduce-scatter.10.cloned.1.call-update) | async-done | bytes 294928
  287.0 1.2 copy.62
  288.1 0.1 multiply_convert_fusion.4
  288.2 0.9 copy.51
  289.1 101.7 %reduce-scatter.8.cloned.1.call-done = bf16[384,1152]{1,0:T(8,128)(2,1)} async-done(((bf16[6144,1152]{1,0:T(8,128)(2,1)}), bf16[384,1152]{1,0:T(8,128)(2,1)}) %reduce-scatter.8.cloned.1.call-update) | async-done | bytes 884752 | tf_op jit(solution)/shard_map/reduce_scatter | solution.py:105
  390.8 1.3 multiply_convert_fusion.1
  392.1 0.9 copy.49
  393.0 2.2 copy.50
  (35 shorter events, 0.2 us)
Async XLA Ops:
  7.2 57.9 %all-gather.5.cloned.1.call-start = ((), (), s32[]{:S(2)}) async-start(), calls=%async_computation.7 | async-start | bytes 3538944 | tf_op jit(solution)/shard_map/all_gather | solution.py:74
  13.1 13.9 %all-to-all-start = ((s32[16,1,32]{2,1,0:T(1,128)}), s32[16,1,32]{2,1,0:T(1,128)S(1)}, u32[]{:S(2)}, u32[]{:S(2)}) async-start(s32[16,1,32]{2,1,0:T(1,128)} %all_to_all.9), calls=%async_computation | async-start | bytes 16384 | tf_op jit(solution)/shard_map/all_to_all | solution.py:63
  27.0 15.6 %all-to-all-start.1 = ((bf16[16,32,768]{2,1,0:T(8,128)(2,1)}), bf16[16,32,768]{2,1,0:T(8,128)(2,1)S(1)}, u32[]{:S(2)}, u32[]{:S(2)}) async-start(bf16[16,32,768]{2,1,0:T(8,128)(2,1)} %bitcast.3), calls=%async_computation.1 | async-start | bytes 1572864 | tf_op jit(solution)/shard_map/all_to_all | solution.py:56
  30.6 45.4 %all-gather.3.cloned.1.call-start = ((), (), s32[]{:S(2)}) async-start(), calls=%async_computation.5 | async-start | bytes 3538944 | tf_op jit(solution)/shard_map/all_gather | solution.py:73
  45.9 19.0 %copy-start.7 = (f32[2,128]{1,0:T(2,128)S(1)}, f32[2,128]{1,0:T(2,128)}, u32[]{:S(2)}) copy-start(f32[2,128]{1,0:T(2,128)} %param.15) | copy-start | bytes 3076
  45.9 19.0 %copy-start.6 = (s32[256]{0:T(256)S(1)}, s32[256]{0:T(256)}, u32[]{:S(2)}) copy-start(s32[256]{0:T(256)} %param.12) | copy-start | bytes 3076
  45.9 123.0 %all-reduce.5.cloned.1.call-start = ((), (), s32[]{:S(2)}) async-start(), calls=%async_computation.8 | async-start | bytes 6291456 | tf_op jit(solution)/shard_map/psum | solution.py:95
  70.3 9.5 %copy-start.5 = (f32[6144]{0:T(1024)S(1)}, f32[6144]{0:T(1024)}, u32[]{:S(2)}) copy-start(f32[6144]{0:T(1024)} %param.13) | copy-start | bytes 73732
  76.0 2.8 copy-start
  87.2 2.5 copy-start.1
  87.9 1.1 copy-start.4
  101.8 103.6 %reduce-scatter.6.cloned.1.call-start = ((), (), s32[]{:S(2)}) async-start(), calls=%async_computation.6 | async-start | bytes 3538944 | tf_op jit(solution)/shard_map/reduce_scatter | solution.py:86
  109.6 177.4 %reduce-scatter.10.cloned.1.call-start = ((), (), s32[]{:S(2)}) async-start(), calls=%async_computation.10 | async-start | bytes 5013504
  121.9 268.9 %reduce-scatter.8.cloned.1.call-start = ((), (), s32[]{:S(2)}) async-start(), calls=%async_computation.9 | async-start | bytes 15040512 | tf_op jit(solution)/shard_map/reduce_scatter | solution.py:105
  130.9 74.5 %copy-start.2 = (bf16[256,768]{1,0:T(8,128)(2,1)S(1)}, bf16[256,768]{1,0:T(8,128)(2,1)}, u32[]{:S(2)}) copy-start(bf16[256,768]{1,0:T(8,128)(2,1)} %scatter_custom_fusion.2) | copy-start | bytes 1179652
  168.9 4.2 %copy-start.3 = (bf16[256,768]{1,0:T(8,128)(2,1)S(1)}, bf16[256,768]{1,0:T(8,128)(2,1)}, u32[]{:S(2)}) copy-start(bf16[256,768]{1,0:T(8,128)(2,1)} %param.17) | copy-start | bytes 1179652
Sparse Core Ops, SparseCore 0:
  9.7 31.5 all-gather.4
  46.0 29.9 all-gather.2
  102.0 66.9 all-reduce.4
  171.2 34.1 reduce-scatter.5
  208.6 78.3 reduce-scatter.9
  290.3 100.3 reduce-scatter.7
where the time goes:
time: 403 us; the launch traced here: 402 us
  waiting for transfers between devices  271 us (67%)
  matrix products  47.5 us (12%)
  local copies, waits for them, and re-layouts  40.4 us (10%)
  other arithmetic  16.8 us (4%)
  between operations  14.4 us (4%)
  starting transfers between devices  11.8 us (3%)
    reduce_scatter x1, waiting for transfers between devices, shards(): lax.psum_scatter(contract_rows(normed, d_proj_bf).astype(jnp.bfloat16), '...  102 us
    unnamed x7, waiting for transfers between devices  80.5 us
    psum x1, waiting for transfers between devices, shards(): d_normed = lax.psum(d_part.astype(jnp.bfloat16), 'mp').astype(jnp.float32)  38 us
    reduce_scatter x1, waiting for transfers between devices, shards(): lax.psum_scatter(contract_cols(heads_out, w_out).astype(jnp.bfloat16), 'm...  31.3 us
    unnamed x21, local copies, waits for them, and re-layouts  30 us
    dot_general x2, matrix products, contract_cols(): lax.dot_general(left, right, (((1,), (1,)), ((), ())), preferred_element_...  17.1 us
    dot_general x2, matrix products, contract_rows(): lax.dot_general(left, right, (((0,), (0,)), ((), ())), preferred_element_...  14.4 us
    all_to_all x1, waiting for transfers between devices, shards(): lax.all_to_all(outbox.reshape(groups, slot_size, part_width), 'dp', split...  10.6 us
  transfers between devices with their start and end apart: 8, of which 7 were waited for; matrix products, arithmetic and copies ran while one was open for 18% of the time, Pallas kernels for 0%

commit v1 on v0

--- a/solution.py
+++ b/solution.py
@@ -1,3 +1,4 @@
+import functools
 import math
 import jax
 import jax.numpy as jnp
@@ -5,6 +6,14 @@
 from jax.sharding import PartitionSpec as P
 
 DH = 128
+
+
+def rest_hubs(tile_in, bus_axis):
+    earlier = lax.all_gather(tile_in, bus_axis)
+    return jnp.sum(earlier, axis=0)
+
+
+cycles_mix = functools.partial(rest_hubs, bus_axis="mp")
 
 
 def norm_heads(values, gain):
@@ -92,7 +101,7 @@
     d_proj_bf = d_projected.astype(jnp.bfloat16).reshape(group_rows, 3 * local_width)
     d_part = contract_cols(d_proj_bf, w_flat)
     my_index = lax.axis_index("mp")
-    d_normed = lax.psum(d_part.astype(jnp.bfloat16), "mp").astype(jnp.float32)
+    d_normed = cycles_mix(d_part.astype(jnp.bfloat16)).astype(jnp.float32)
     d_unit = d_normed * ln_gain
     d_full = rstd * (
         d_unit

time: 403 us -> 476 us (1.18)
  waiting for transfers between devices: 271 us -> 323 us
  other arithmetic: 16.8 us -> 33.4 us
    all_gather x0 -> x1, waiting for transfers between devices: none -> 115 us  [rest_hubs(): earlier = lax.all_gather(tile_in, bus_axis)]
    psum x1 -> x0, waiting for transfers between devices: 38 us -> none  [shards(): d_normed = lax.psum(d_part.astype(jnp.bfloat16), 'mp').astype(jnp.float32)]
    reduce_scatter x1, waiting for transfers between devices: 31.3 us -> 0.02 us  [shards(): lax.psum_scatter(contract_cols(heads_out, w_out).astype(jnp.bfloat16), 'm...]
    reduce_sum x0 -> x1, other arithmetic: none -> 15.8 us  [rest_hubs(): return jnp.sum(earlier, axis=0)]
    all_gather x1, waiting for transfers between devices: 0.02 us -> 13 us  [shards(): lax.all_gather(cotangent, 'mp', axis=1, tiled=True)]
    unnamed x7, waiting for transfers between devices: 80.5 us -> 71.1 us
    all_gather x1, waiting for transfers between devices: 5.52 us -> 10.3 us  [shards(): lax.all_gather(packed, 'mp', axis=1, tiled=True)]
    unnamed x21 -> x33, local copies, waits for them, and re-layouts: 30 us -> 32.4 us
  transfers between devices with their start and end apart: 8 -> 8, of which waited for: 7 -> 7; matrix products, arithmetic and copies ran while one was open for 18% -> 20% of each run, Pallas kernels for 0% -> 0%
where the time goes in v1:
time: 476 us; the launch traced here: 475 us
  waiting for transfers between devices  323 us (68%)
  matrix products  46.4 us (10%)
  local copies, waits for them, and re-layouts  45.1 us (9%)
  other arithmetic  33.4 us (7%)
  between operations  14.4 us (3%)
  starting transfers between devices  12.1 us (3%)
    all_gather x1, waiting for transfers between devices, rest_hubs(): earlier = lax.all_gather(tile_in, bus_axis)  115 us
    reduce_scatter x1, waiting for transfers between devices, shards(): lax.psum_scatter(contract_rows(normed, d_proj_bf).astype(jnp.bfloat16), '...  100 us
    unnamed x7, waiting for transfers between devices  71.1 us
    unnamed x33, local copies, waits for them, and re-layouts  32.4 us
    reduce_sum x1, other arithmetic, rest_hubs(): return jnp.sum(earlier, axis=0)  15.8 us
    dot_general x2, matrix products, contract_cols(): lax.dot_general(left, right, (((1,), (1,)), ((), ())), preferred_element_...  14.8 us
    dot_general x2, matrix products, contract_rows(): lax.dot_general(left, right, (((0,), (0,)), ((), ())), preferred_element_...  13.3 us
    all_gather x1, waiting for transfers between devices, shards(): lax.all_gather(cotangent, 'mp', axis=1, tiled=True)  13 us
  transfers between devices with their start and end apart: 8, of which 7 were waited for; matrix products, arithmetic and copies ran while one was open for 20% of the time, Pallas kernels for 0%

profile of v1, /device:TPU:1, one launch (start us, length us, event | category | flops | bytes accessed | tf_op | source)
XLA Modules:
  0.0 474.7 jit_solution(1662176876880027350)
XLA Ops:
  7.2 0.7 fusion.32
  7.9 0.6 reduce-window.6
  8.4 0.2 slice_reduce_fusion.2
  8.6 0.8 fusion.31
  9.4 0.7 compare_select_fusion.1
  10.1 1.6 scatter_custom_fusion
  11.7 0.7 all_to_all.9
  12.3 7.6 %all-to-all-start = ((s32[16,1,32]{2,1,0:T(1,128)}), s32[16,1,32]{2,1,0:T(1,128)S(1)}, u32[]{:S(2)}, u32[]{:S(2)}) async-start(s32[16,1,32]{2,1,0:T(1,128)} %all_to_all.9), calls=%async_computation | async-start | bytes 16384 | tf_op jit(solution)/shard_map/all_to_all | solution.py:72
  19.9 3.0 scatter_custom_fusion.1
  23.0 3.3 all-to-all-done
  26.3 3.6 all-to-all-start.1
  29.9 0.0 all-gather.5.cloned.1.call-start
  29.9 0.5 broadcast.243
  30.5 0.7 reduce.8
  31.1 0.1 reshape.195
  31.2 10.6 %all-to-all-done.1 = bf16[16,32,768]{2,1,0:T(8,128)(2,1)S(1)} async-done(((bf16[16,32,768]{2,1,0:T(8,128)(2,1)}), bf16[16,32,768]{2,1,0:T(8,128)(2,1)S(1)}, u32[]{:S(2)}, u32[]{:S(2)}) %all-to-all-start.1) | async-done | bytes 786464 | tf_op jit(solution)/shard_map/all_to_all | solution.py:65
  41.8 3.3 scatter_custom_fusion.2
  45.2 0.7 all-gather.7.cloned.1.call-update
  46.0 0.2 reduce-scatter.6.cloned.1.call-start
  46.2 18.6 %copy.39 = bf16[6144,3,384]{0,2,1:T(8,128)(2,1)} copy(bf16[6144,3,384]{2,0,1:T(8,128)(2,1)} %param.14) | data formatting | bytes 28311552 | tf_op args[5]
  64.8 0.1 broadcast_compare_fusion
  65.0 10.3 %all-gather.5.cloned.1.call-done = bf16[256,6144]{1,0:T(8,128)(2,1)} async-done(((bf16[256,768]{1,0:T(8,128)(2,1)}), bf16[256,6144]{1,0:T(8,128)(2,1)}) %all-gather.5.cloned.1.call-update) | async-done | bytes 3145744 | tf_op jit(solution)/shard_map/all_gather | solution.py:82
  75.3 2.5 convert_reduce_fusion
  77.8 0.3 copy-done
  78.1 1.0 fusion.4
  79.1 7.5 %fusion.5 = f32[256,3,3,128]{0,3,2,1:T(8,128)S(1)} fusion(bf16[3,3,128,6144]{3,2,1,0:T(8,128)(2,1)} %bitcast.124, f32[6144]{0:T(1024)S(1)} %copy-done.8, bf16[256,6144]{1,0:T(8,128)(2,1)S(1)} %copy-done, f32[256]{0:T(256)S(1)} %add_rsqrt_fusion, f32[256]{0:T(256)S(1)} %broadcast_multiply_fusion.4), kind=kOutput, calls=%fused_computation.17 | convolution fusion | flops 3631742976 | bytes 18507776 | tf_op jit(solution)/shard_map/dot_general | solution.py:91
  86.6 0.1 slice_reduce_fusion
  86.7 0.1 multiply_reduce_fusion.4
  86.8 0.5 select_reduce_fusion
  87.3 0.4 copy-done.1
  87.7 0.3 convolution_convert_fusion.6
  87.9 0.2 copy-done.6
  88.2 3.6 convolution_convert_fusion.2
  91.8 0.0 reduce-scatter.10.cloned.1.call-start
  91.8 13.0 %all-gather.7.cloned.1.call-done = bf16[256,6144]{1,0:T(8,128)(2,1)} async-done(((bf16[256,768]{1,0:T(8,128)(2,1)}), bf16[256,6144]{1,0:T(8,128)(2,1)}) %all-gather.7.cloned.1.call-update) | async-done | bytes 3145744 | tf_op jit(solution)/shard_map/all_gather | solution.py:83
  104.9 5.4 %fusion.1 = bf16[6144,384]{0,1:T(8,128)(2,1)} fusion(bf16[256,384]{0,1:T(8,128)(2,1)S(1)} %bitcast.134, bf16[256,6144]{1,0:T(8,128)(2,1)} %all-gather.7.cloned.1.call-done), kind=kOutput, calls=%fused_computation.9 | convolution fusion | flops 1210318848 | bytes 8060928 | tf_op jit(solution)/shard_map/dot_general | solution.py:43
  110.3 6.7 %copy.61 = bf16[6144,384]{1,0:T(8,128)(2,1)} copy(bf16[6144,384]{0,1:T(8,128)(2,1)} %fusion.1) | data formatting | bytes 9437184
  117.0 0.3 reduce-scatter.8.cloned.1.call-start
  117.3 5.8 %convolution_convert_fusion.5 = bf16[256,384]{1,0:T(8,128)(2,1)} fusion(bf16[256,6144]{1,0:T(8,128)(2,1)} %all-gather.7.cloned.1.call-done, bf16[6144,384]{1,0:T(8,128)(2,1)} %param.16), kind=kOutput, calls=%fused_computation.27 | convolution fusion | flops 1208057856 | bytes 8060928 | tf_op jit(solution)/shard_map/dot_general | solution.py:99
  123.1 1.1 copy.43
  124.2 1.8 multiply_reduce_fusion.1
  126.0 1.8 multiply_reduce_fusion.3
  127.8 0.4 fusion.28
  128.3 0.2 add_bitcast_fusion.1
  128.4 0.3 fusion.16
  128.8 0.1 add_bitcast_fusion
  128.8 0.1 add_convert_fusion
  128.9 0.8 copy-done.4
  129.7 7.8 %convolution_convert_fusion = bf16[6144,1152]{1,0:T(8,128)(2,1)} fusion(bf16[256,1152]{0,1:T(8,128)(2,1)S(1)} %bitcast.128, f32[6144]{0:T(1024)S(1)} %copy-done.8, bf16[256,6144]{1,0:T(8,128)(2,1)S(1)} %copy-done, f32[256]{0:T(256)S(1)} %add_rsqrt_fusion, f32[256]{0:T(256)S(1)} %broadcast_multiply_fusion.4), kind=kOutput, calls=%fused_computation.3 | convolution fusion | flops 3638820864 | bytes 17917952 | tf_op jit(solution)/shard_map/dot_general | solution.py:43
  137.6 0.3 all-gather.9.cloned.1.call-start
  137.9 11.3 %fusion = bf16[256,6144]{1,0:T(8,128)(2,1)} fusion(bf16[256,3,384]{0,2,1:T(8,128)(2,1)} %bitcast.129, bf16[6144,3,384]{2,0,1:T(8,128)(2,1)} %param.14), kind=kOutput, calls=%fused_computation.8 | convolution fusion | flops 3625451520 | bytes 17891328 | tf_op jit(solution)/shard_map/dot_general | solution.py:49
  149.3 1.8 add_convert_fusion.1
  151.1 70.3 %reduce-scatter.10.cloned.1.call-done = bf16[384,384]{1,0:T(8,128)(2,1)} async-done(((bf16[6144,384]{1,0:T(8,128)(2,1)}), bf16[384,384]{1,0:T(8,128)(2,1)}) %reduce-scatter.10.cloned.1.call-update) | async-done | bytes 294928
  221.4 1.2 copy.62
  222.6 0.8 multiply_convert_fusion.4
  223.4 1.8 copy.51
  225.2 100.1 %reduce-scatter.8.cloned.1.call-done = bf16[384,1152]{1,0:T(8,128)(2,1)} async-done(((bf16[6144,1152]{1,0:T(8,128)(2,1)}), bf16[384,1152]{1,0:T(8,128)(2,1)}) %reduce-scatter.8.cloned.1.call-update) | async-done | bytes 884752 | tf_op jit(solution)/shard_map/reduce_scatter | solution.py:114
  325.3 2.2 multiply_convert_fusion.1
  327.5 2.3 copy.49
  329.8 2.3 copy.50
  332.1 114.8 %all-gather.9.cloned.1.call-done = bf16[2048,6144]{1,0:T(8,128)(2,1)} async-done(((bf16[256,6144]{1,0:T(8,128)(2,1)}), bf16[2048,6144]{1,0:T(8,128)(2,1)}) %all-gather.9.cloned.1.call-update) | async-done | bytes 25165840 | tf_op jit(solution)/shard_map/all_gather | solution.py:12
  446.9 15.8 %reduce_sum.180 = bf16[256,6144]{1,0:T(8,128)(2,1)} reduce(bf16[8,256,6144]{2,1,0:T(8,128)(2,1)} %bitcast.123, bf16[]{:T(256)} %constant.20.clone.1), dimensions={0}, to_apply=%region_19.20 | reduce | flops 11010048 | bytes 28311554 | tf_op jit(solution)/shard_map/reduce_sum | solution.py:13
  462.7 4.1 fusion.7
  466.9 1.0 fusion.20
  (49 shorter events, 0.4 us)
Async XLA Ops:
  12.3 13.9 %all-to-all-start = ((s32[16,1,32]{2,1,0:T(1,128)}), s32[16,1,32]{2,1,0:T(1,128)S(1)}, u32[]{:S(2)}, u32[]{:S(2)}) async-start(s32[16,1,32]{2,1,0:T(1,128)} %all_to_all.9), calls=%async_computation | async-start | bytes 16384 | tf_op jit(solution)/shard_map/all_to_all | solution.py:72
  26.3 15.6 %all-to-all-start.1 = ((bf16[16,32,768]{2,1,0:T(8,128)(2,1)}), bf16[16,32,768]{2,1,0:T(8,128)(2,1)S(1)}, u32[]{:S(2)}, u32[]{:S(2)}) async-start(bf16[16,32,768]{2,1,0:T(8,128)(2,1)} %bitcast.3), calls=%async_computation.1 | async-start | bytes 1572864 | tf_op jit(solution)/shard_map/all_to_all | solution.py:65
  29.9 45.4 %all-gather.5.cloned.1.call-start = ((), (), s32[]{:S(2)}) async-start(), calls=%async_computation.5 | async-start | bytes 3538944 | tf_op jit(solution)/shard_map/all_gather | solution.py:82
  45.2 59.7 %all-gather.7.cloned.1.call-start = ((), (), s32[]{:S(2)}) async-start(), calls=%async_computation.7 | async-start | bytes 3538944 | tf_op jit(solution)/shard_map/all_gather | solution.py:83
  45.9 18.9 %copy-start.11 = (f32[2,128]{1,0:T(2,128)S(1)}, f32[2,128]{1,0:T(2,128)}, u32[]{:S(2)}) copy-start(f32[2,128]{1,0:T(2,128)} %param.15) | copy-start | bytes 3076
  46.0 18.9 %copy-start.10 = (s32[256]{0:T(256)S(1)}, s32[256]{0:T(256)}, u32[]{:S(2)}) copy-start(s32[256]{0:T(256)} %param.12) | copy-start | bytes 3076
  46.0 103.3 %reduce-scatter.6.cloned.1.call-start = ((), (), s32[]{:S(2)}) async-start(), calls=%async_computation.6 | async-start | bytes 3538944 | tf_op jit(solution)/shard_map/reduce_scatter | solution.py:95
  64.8 14.3 %copy-start.8 = (f32[6144]{0:T(1024)S(1)}, f32[6144]{0:T(1024)}, u32[]{:S(2)}) copy-start(f32[6144]{0:T(1024)} %param.13) | copy-start | bytes 73732
  75.3 2.8 copy-start
  79.1 9.1 %slice-start = ((s8[4718592]{0:T(1024)(128)(4,1)}), s8[4194304]{0:T(1024)(128)(4,1)S(1)}, s32[]{:S(2)}) async-start(s8[4718592]{0:T(1024)(128)(4,1)} %bitcast.125), calls=%async_computation.11 | async-start | bytes 8388608
  79.1 9.1 %slice-start.1 = ((s8[4718592]{0:T(1024)(128)(4,1)}), s8[524288]{0:T(1024)(128)(4,1)S(1)}, s32[]{:S(2)}) async-start(s8[4718592]{0:T(1024)(128)(4,1)} %bitcast.125), calls=%async_computation.12 | async-start | bytes 1048576
  86.6 1.1 copy-start.1
  87.3 0.9 copy-start.6
  91.8 129.6 %reduce-scatter.10.cloned.1.call-start = ((), (), s32[]{:S(2)}) async-start(), calls=%async_computation.10 | async-start | bytes 5013504
  117.0 208.3 %reduce-scatter.8.cloned.1.call-start = ((), (), s32[]{:S(2)}) async-start(), calls=%async_computation.8 | async-start | bytes 15040512 | tf_op jit(solution)/shard_map/reduce_scatter | solution.py:114
  124.2 3.6 copy-start.2
  124.2 3.6 copy-start.7
  128.9 0.8 copy-start.4
  137.6 309.3 %all-gather.9.cloned.1.call-start = ((), (), s32[]{:S(2)}) async-start(), calls=%async_computation.9 | async-start | bytes 28311552 | tf_op jit(solution)/shard_map/all_gather | solution.py:12
  137.9 11.3 %copy-start.3 = (bf16[256,768]{1,0:T(8,128)(2,1)S(1)}, bf16[256,768]{1,0:T(8,128)(2,1)}, u32[]{:S(2)}) copy-start(bf16[256,768]{1,0:T(8,128)(2,1)} %scatter_custom_fusion.2) | copy-start | bytes 1179652
  446.9 15.8 %copy-start.9 = (f32[6144]{0:T(1024)S(1)}, f32[6144]{0:T(1024)}, u32[]{:S(2)}) copy-start(f32[6144]{0:T(1024)} %param.13) | copy-start | bytes 73732
  462.7 4.2 copy-start.5
Sparse Core Ops, SparseCore 0:
  45.3 29.9 all-gather.4
  77.0 27.8 all-gather.6
  107.3 32.1 reduce-scatter.5
  142.7 78.7 reduce-scatter.9
  224.8 100.4 reduce-scatter.7
  327.0 119.8 all-gather.8
